TPU v7x, 512 devices: a whole 4x4x16 slice. The times are simulated.
512 devices in a mesh: guide: 2 (over x_lo), seq: 32 (over x_hi, z), blk: 8 (over y, core).
Axes of the slice: x: 4 (x_hi: 2, x_lo: 2; x = x_hi * 2 + x_lo), y: 4, z: 16, core: 2. Of those that a mesh axis runs over, the one named last changes fastest.
Arguments:
- img_hidden: bfloat16 [2, 2, 2048, 3072], P('guide', None, 'seq', 'blk'), may hold values from -6 to 6
- img_query: bfloat16 [2, 2, 2048, 3072], P('guide', None, 'seq', 'blk')
- img_key: bfloat16 [2, 2, 2048, 3072], P('guide', None, 'seq', 'blk')
- img_value: bfloat16 [2, 2, 2048, 3072], P('guide', None, 'seq', 'blk'), may hold values from -6 to 6
- txt_key: bfloat16 [2, 2, 512, 3072], P('guide', None, 'seq', 'blk'), may hold values from -6 to 6
- txt_value: bfloat16 [2, 2, 512, 3072], P('guide', None, 'seq', 'blk'), may hold values from -6 to 6
- query_gain: float32 [128], replicated
- key_gain: float32 [2, 128], replicated
- gate: float32 [2, 2, 3072], P('guide', None, 'blk'), may hold values from -4 to 4
- proj_weight: bfloat16 [3072, 3072], P('blk'), may hold values from -0.15625 to 0.15625
- proj_bias: float32 [3072], P('blk'), may hold values from -3 to 3
- guidance: float32 [2], replicated, may hold values from 1.5 to 5
- text_len: int32 [2], replicated, may hold values from 1 to 512, as said below
- step_index: int32 [1], replicated, may hold values from 0 to 7
- latent: bfloat16 [2, 2048, 3072], P('guide', 'seq', 'blk'), may hold values from -6 to 6
Outputs:
- guided: bfloat16 [2, 2048, 3072], P('guide', 'seq', 'blk')
- next_state: bfloat16 [2, 2048, 3072], P('guide', 'seq', 'blk')
Inputs may be any that keep to these rules, and one draw needn't show every extreme that they name: `text_len`: some prompt has all 512 text slots live.
All inputs are finite; a program needn't handle non-finite values.
Results may differ from a plain program's by a relative error of at most 0.0095.
Values may be sent and summed in bfloat16 or wider, within the bound.
No kernel may reach another device: no remote copies, remote signals or barrier semaphores. Data moves between devices by JAX's collectives and lax.ppermute only.
A program may use at most 64 MiB of HBM per device.

v0:
```python
import jax
import jax.numpy as jnp
from jax import lax
from jax.sharding import PartitionSpec as P

HD = 128
GRID = 64
STEPS = 8


def rope_angles(positions):
    first = HD // 8
    second = (HD - first) // 2
    freqs = 10000.0 ** (-jnp.arange(0, second, 2).astype(jnp.float32) / second)
    rows = (positions // GRID).astype(jnp.float32)
    cols = (positions % GRID).astype(jnp.float32)
    zeros = jnp.zeros((positions.shape[0], first // 2), jnp.float32)
    return jnp.concatenate([zeros, rows[:, None] * freqs, cols[:, None] * freqs], -1)


def rotate(values, angles):
    pairs = values.reshape(values.shape[:-1] + (HD // 2, 2))
    cosine = jnp.cos(angles)[None, :, None, :]
    sine = jnp.sin(angles)[None, :, None, :]
    first = pairs[..., 0] * cosine - pairs[..., 1] * sine
    second = pairs[..., 0] * sine + pairs[..., 1] * cosine
    return jnp.stack([first, second], -1).reshape(values.shape)


def normed(values, gain_row):
    heads = values.astype(jnp.float32).reshape(
        values.shape[0], values.shape[1], values.shape[2] // HD, HD
    )
    return heads / jnp.sqrt(jnp.mean(heads * heads, -1, keepdims=True) + 1e-06) * gain_row


def shards(
    img_hidden,
    img_query,
    img_key,
    img_value,
    txt_key,
    txt_value,
    query_gain,
    key_gain,
    gate,
    proj_weight,
    proj_bias,
    guidance,
    text_len,
    step_index,
    latent,
):
    prompts = img_query.shape[1]
    img_here = img_query.shape[2]
    txt_here = txt_key.shape[2]
    width_here = img_query.shape[3]
    heads_here = width_here // HD
    slot_here = img_here + txt_here
    positions = lax.axis_index("seq") * img_here + jnp.arange(img_here)
    angles = rope_angles(positions)
    queries = rotate(normed(img_query[0], query_gain), angles).astype(jnp.bfloat16)
    keys_img = rotate(normed(img_key[0], key_gain[0]), angles).astype(jnp.bfloat16)
    keys_txt = normed(txt_key[0], key_gain[1]).astype(jnp.bfloat16)
    keys_local = jnp.concatenate([keys_txt, keys_img], 1).reshape(prompts, slot_here, width_here)
    values_local = jnp.concatenate([txt_value[0], img_value[0]], 1)
    running = jnp.full((prompts, img_here, heads_here), -1e30, jnp.float32)
    key_piece = lax.all_gather(keys_local, "seq", axis=1, tiled=True)
    value_piece = lax.all_gather(values_local, "seq", axis=1, tiled=True)
    count = key_piece.shape[1]
    index = jnp.arange(count)
    device = index // slot_here
    within = index % slot_here
    text_pos = device * txt_here + within
    live = (within >= txt_here)[None, :] | (text_pos[None, :] < text_len[:, None])
    key_heads = key_piece.reshape(prompts, count, heads_here, HD)
    value_heads = value_piece.reshape(prompts, count, heads_here, HD)
    scores = jnp.einsum(
        "pqhd,pkhd->pqhk", queries, key_heads, preferred_element_type=jnp.float32
    ) * HD ** (-0.5)
    mask = live[:, None, None, :]
    scores = jnp.where(mask, scores, -1e30)
    newest = jnp.maximum(running, jnp.max(scores, -1))
    expo = jnp.where(mask, jnp.exp(scores - newest[..., None]), 0.0)
    total = jnp.sum(expo, -1)
    accum = jnp.einsum(
        "pqhk,pkhd->pqhd",
        expo.astype(jnp.bfloat16),
        value_heads,
        preferred_element_type=jnp.float32,
    )
    running, total, accum = (newest, total, accum)
    attn = (accum / total[..., None]).astype(jnp.bfloat16).reshape(prompts * img_here, width_here)
    partial_value = jnp.dot(attn, proj_weight, preferred_element_type=jnp.float32)
    proj = lax.psum_scatter(
        partial_value.astype(jnp.bfloat16), "blk", scatter_dimension=1, tiled=True
    ).astype(jnp.float32)
    proj = (proj + proj_bias).reshape(prompts, img_here, width_here)
    layer_out = (img_hidden[0].astype(jnp.float32) + gate[0][:, None, :] * proj).astype(
        jnp.bfloat16
    )
    both_halves = lax.all_to_all(layer_out[None], "guide", split_axis=1, concat_axis=0, tiled=True)
    cond = both_halves[0].astype(jnp.float32)
    uncond = both_halves[1].astype(jnp.float32)
    own_prompts = cond.shape[0]
    scale_here = lax.dynamic_slice_in_dim(
        guidance, lax.axis_index("guide") * own_prompts, own_prompts, 0
    )
    guided_f = uncond + scale_here[:, None, None] * (cond - uncond)
    index = step_index[0]
    u_now = 1.0 - index.astype(jnp.float32) / STEPS
    u_next = 1.0 - (index + 1).astype(jnp.float32) / STEPS
    step_size = 3.0 * u_next / (1.0 + 2.0 * u_next) - 3.0 * u_now / (1.0 + 2.0 * u_now)
    next_state = (latent.astype(jnp.float32) + step_size * guided_f).astype(jnp.bfloat16)
    return (guided_f.astype(jnp.bfloat16), next_state)


def solution(mesh):
    return jax.shard_map(
        shards,
        mesh=mesh,
        in_specs=(
            P("guide", None, "seq", "blk"),
            P("guide", None, "seq", "blk"),
            P("guide", None, "seq", "blk"),
            P("guide", None, "seq", "blk"),
            P("guide", None, "seq", "blk"),
            P("guide", None, "seq", "blk"),
            P(),
            P(),
            P("guide", None, "blk"),
            P("blk", None),
            P("blk"),
            P(),
            P(),
            P(),
            P("guide", "seq", "blk"),
        ),
        out_specs=(P("guide", "seq", "blk"), P("guide", "seq", "blk")),
        check_vma=False,
    )
```

profile of v0, /device:TPU:4, one launch (start us, length us, event | category | flops | bytes accessed | tf_op | source)
XLA Modules:
  0.0 420.7 jit_solution(10959240967538015908)
XLA Ops:
  7.2 0.6 multiply_power_fusion
  7.8 1.6 convert_multiply_fusion.1
  9.5 1.0 copy.58
  10.5 1.6 convert_multiply_fusion.2
  12.1 1.0 copy.52
  13.1 0.6 fusion.35
  13.7 0.8 slice_bitcast_fusion.2
  14.5 0.1 mul.268
  14.6 1.0 mul.267
  15.6 0.2 reduce_sum.37
  15.9 0.7 copy.54
  16.6 1.0 mul.285
  17.6 0.2 reduce_sum.38
  17.8 0.7 copy.60
  18.5 0.8 mul.286
  19.3 0.7 convert_multiply_fusion
  20.1 0.1 reduce_sum.36
  20.2 0.1 div.91
  20.4 0.2 copy.55
  20.6 0.8 broadcast_multiply_fusion.1
  21.3 0.2 fusion.26
  21.5 1.1 divide_multiply_fusion
  22.7 1.0 subtract_convert_fusion
  23.7 0.5 pad_maximum_fusion
  24.2 0.1 pad_maximum_fusion.1
  24.4 0.8 copy.56
  25.2 0.1 copy.82
  25.4 0.8 copy.83
  26.1 0.8 pad_maximum_fusion.3
  27.0 0.5 pad_maximum_fusion.2
  27.6 0.7 compare_or_fusion
  28.3 161.3 %all-gather.5.cloned.1.call-done = bf16[2,2560,384]{2,0,1:T(2,128)(2,1)} async-done(((bf16[2,80,384]{2,0,1:T(2,128)(2,1)}), bf16[2,2560,384]{2,0,1:T(2,128)(2,1)}) %all-gather.5.cloned.1.call-update) | async-done | bytes 3932176 | tf_op jit(solution)/shard_map/all_gather | solution.py:68
  189.6 10.5 %copy.57 = bf16[2,2560,384]{1,2,0:T(8,128)(2,1)} copy(bf16[2,2560,384]{2,0,1:T(2,128)(2,1)} %all-gather.5.cloned.1.call-done) | data formatting | bytes 7864320 | tf_op jit(solution)/shard_map/all_gather | solution.py:68
  200.1 3.2 fusion.38
  203.4 1.9 copy-done.1
  205.2 0.9 fusion.2
  206.1 143.7 %all-gather.3.cloned.1.call-done = bf16[2,2560,384]{2,0,1:T(2,128)(2,1)} async-done(((bf16[2,80,384]{2,0,1:T(2,128)(2,1)}), bf16[2,2560,384]{2,0,1:T(2,128)(2,1)}) %all-gather.3.cloned.1.call-update) | async-done | bytes 3932176 | tf_op jit(solution)/shard_map/all_gather | solution.py:69
  349.8 10.5 %copy.51 = bf16[2,2560,384]{1,2,0:T(8,128)(2,1)} copy(bf16[2,2560,384]{2,0,1:T(2,128)(2,1)} %all-gather.3.cloned.1.call-done) | data formatting | bytes 7864320 | tf_op jit(solution)/shard_map/all_gather | solution.py:69
  360.3 4.8 %fusion.15 = bf16[2,64,3,128]{3,1,2,0:T(8,128)(2,1)S(1)} fusion(bf16[2,2560,3,128]{1,3,2,0:T(8,128)(2,1)} %bitcast.73, f32[2,64,3,2560]{3,1,2,0:T(8,128)} %copy-done.1, f32[2,64,3]{1,2,0:T(4,128)S(1)} %broadcast_maximum_fusion, pred[2,2560]{1,0:T(4,128)(4,1)S(1)} %compare_or_fusion, f32[2,64,3]{1,2,0:T(4,128)S(1)} %fusion.2), kind=kOutput, calls=%fused_computation.13 | convolution fusion | flops 254705664 | bytes 7970816 | tf_op jit(solution)/shard_map/pqhk,pkhd->pqhd/dot_general | solution.py:86
  365.3 0.6 convolution_convert_fusion
  365.9 1.2 copy.69
  367.1 36.4 %reduce-scatter.4.cloned.1.call-done = bf16[384,128]{1,0:T(8,128)(2,1)} async-done(((bf16[3072,128]{1,0:T(8,128)(2,1)}), bf16[384,128]{1,0:T(8,128)(2,1)}) %reduce-scatter.4.cloned.1.call-update) | async-done | bytes 98320
  403.5 1.0 copy.70
  404.5 0.7 add_convert_fusion
  405.2 3.3 all-to-all-start
  409.2 0.6 dynamic_slice.3
  409.9 2.9 all-to-all-done
  412.8 1.3 add_convert_fusion.3
  (37 shorter events, 0.5 us)
Async XLA Ops:
  7.2 358.1 %copy-start = (bf16[384,3072]{1,0:T(8,128)(2,1)S(1)}, bf16[384,3072]{1,0:T(8,128)(2,1)}, u32[]{:S(2)}) copy-start(bf16[384,3072]{1,0:T(8,128)(2,1)} %param.24) | copy-start | bytes 7077892
  7.2 13.2 %copy-start.4 = (bf16[1,2,16,384]{3,2,1,0:T(8,128)(2,1)S(1)}, bf16[1,2,16,384]{3,2,1,0:T(8,128)(2,1)}, u32[]{:S(2)}) copy-start(bf16[1,2,16,384]{3,2,1,0:T(8,128)(2,1)} %param.19) | copy-start | bytes 73732
  7.2 182.4 %all-gather.5.cloned.1.call-start = ((), (), s32[]{:S(2)}) async-start(), calls=%async_computation.3 | async-start | bytes 4055040 | tf_op jit(solution)/shard_map/all_gather | solution.py:68
  17.8 7.4 %copy-start.2 = (bf16[1,2,64,384]{3,2,1,0:T(8,128)(2,1)S(1)}, bf16[1,2,64,384]{3,2,1,0:T(8,128)(2,1)}, u32[]{:S(2)}) copy-start(bf16[1,2,64,384]{3,2,1,0:T(8,128)(2,1)} %param.18) | copy-start | bytes 294916
  25.2 324.6 %all-gather.3.cloned.1.call-start = ((), (), s32[]{:S(2)}) async-start(), calls=%async_computation.2 | async-start | bytes 4055040 | tf_op jit(solution)/shard_map/all_gather | solution.py:69
  27.0 376.5 %reduce-scatter.4.cloned.1.call-start = ((), (), s32[]{:S(2)}) async-start(), calls=%async_computation.4 | async-start | bytes 884736
  203.3 1.9 copy-start.1
  365.1 39.4 %copy-start.7 = (f32[384]{0:T(512)S(1)}, f32[384]{0:T(512)}, u32[]{:S(2)}) copy-start(f32[384]{0:T(512)} %param.25) | copy-start | bytes 4612
  365.1 39.4 %copy-start.3 = (bf16[1,2,64,384]{3,2,1,0:T(8,128)(2,1)S(1)}, bf16[1,2,64,384]{3,2,1,0:T(8,128)(2,1)}, u32[]{:S(2)}) copy-start(bf16[1,2,64,384]{3,2,1,0:T(8,128)(2,1)} %param.15) | copy-start | bytes 294916
  365.2 39.4 %copy-start.6 = (f32[1,2,384]{2,1,0:T(2,128)S(1)}, f32[1,2,384]{2,1,0:T(2,128)}, u32[]{:S(2)}) copy-start(f32[1,2,384]{2,1,0:T(2,128)} %param.23) | copy-start | bytes 9220
  365.2 44.1 %copy-start.8 = (f32[2]{0:T(128)S(1)}, f32[2]{0:T(128)}, u32[]{:S(2)}) copy-start(f32[2]{0:T(128)} %param.26) | copy-start | bytes 28
  365.2 47.7 %copy-start.5 = (bf16[1,64,384]{2,1,0:T(8,128)(2,1)S(1)}, bf16[1,64,384]{2,1,0:T(8,128)(2,1)}, u32[]{:S(2)}) copy-start(bf16[1,64,384]{2,1,0:T(8,128)(2,1)} %param.29) | copy-start | bytes 147460
  405.2 7.6 %all-to-all-start = ((bf16[1,2,64,384]{3,2,0,1:T(8,128)(2,1)}), bf16[1,2,64,384]{3,2,0,1:T(8,128)(2,1)S(1)}, u32[]{:S(2)}, u32[]{:S(2)}) async-start(bf16[1,2,64,384]{3,2,0,1:T(8,128)(2,1)} %add_convert_fusion), calls=%async_computation | async-start | bytes 196608 | tf_op jit(solution)/shard_map/all_to_all | solution.py:102
Sparse Core Ops, SparseCore 0:
  25.3 164.2 all-gather.4
  192.7 157.0 all-gather.2
  367.2 36.2 reduce-scatter.3
where the time goes:
time: 422 us; the launch traced here: 421 us
  waiting for transfers between devices  344 us (82%)
  local copies, waits for them, and re-layouts  35 us (8%)
  between operations  14.9 us (4%)
  other arithmetic  14.5 us (3%)
  matrix products  8.61 us (2%)
    all_gather x1, waiting for transfers between devices, shards(): key_piece = lax.all_gather(keys_local, 'seq', axis=1, tiled=True)  161 us
    all_gather x1, waiting for transfers between devices, shards(): value_piece = lax.all_gather(values_local, 'seq', axis=1, tiled=True)  144 us
    unnamed x4, waiting for transfers between devices  36.5 us
    all_gather x1, local copies, waits for them, and re-layouts, shards(): value_piece = lax.all_gather(values_local, 'seq', axis=1, tiled=True)  10.5 us
    all_gather x1, local copies, waits for them, and re-layouts, shards(): key_piece = lax.all_gather(keys_local, 'seq', axis=1, tiled=True)  10.5 us
  transfers between devices with their start and end apart: 4, of which 4 were waited for; matrix products, arithmetic and copies ran while one was open for 4% of the time, Pallas kernels for 0%

commit v1 on v0

--- a/solution.py
+++ b/solution.py
@@ -65,8 +65,13 @@
     keys_local = jnp.concatenate([keys_txt, keys_img], 1).reshape(prompts, slot_here, width_here)
     values_local = jnp.concatenate([txt_value[0], img_value[0]], 1)
     running = jnp.full((prompts, img_here, heads_here), -1e30, jnp.float32)
-    key_piece = lax.all_gather(keys_local, "seq", axis=1, tiled=True)
-    value_piece = lax.all_gather(values_local, "seq", axis=1, tiled=True)
+    key_piece, value_piece = jnp.split(
+        lax.all_gather(
+            jnp.concatenate([keys_local, values_local], axis=0), axis_name="seq", tiled=True, axis=1
+        ),
+        [keys_local.shape[0]],
+        axis=0,
+    )
     count = key_piece.shape[1]
     index = jnp.arange(count)
     device = index // slot_here

time: 422 us -> 326 us (0.77)
  waiting for transfers between devices: 344 us -> 230 us
  local copies, waits for them, and re-layouts: 35 us -> 48.3 us
    all_gather x2 -> x1, waiting for transfers between devices: 305 us -> 191 us  [shards(): lax.all_gather(jnp.concatenate([keys_local, values_local], axis=0), axis_...]
    unnamed x22 -> x26, local copies, waits for them, and re-layouts: 4.94 us -> 26.8 us
    all_gather x2 -> x0, local copies, waits for them, and re-layouts: 21.1 us -> none  [the longest x1 10.5 us: shards(): value_piece = lax.all_gather(values_local, 'seq', axis=1, tiled=True)]
    split x0 -> x1, local copies, waits for them, and re-layouts: none -> 11 us  [shards(): jnp.split(lax.all_gather(jnp.concatenate([keys_local, values_local], axis...]
    unnamed x4 -> x3, waiting for transfers between devices: 36.5 us -> 36.3 us
  transfers between devices with their start and end apart: 4 -> 3, of which waited for: 4 -> 3; matrix products, arithmetic and copies ran while one was open for 4% -> 1% of each run, Pallas kernels for 0% -> 0%
where the time goes in v1:
time: 326 us; the launch traced here: 324 us
  waiting for transfers between devices  230 us (71%)
  local copies, waits for them, and re-layouts  48.3 us (15%)
  other arithmetic  18.4 us (6%)
  between operations  15.1 us (5%)
  matrix products  9.21 us (3%)
  starting transfers between devices  3.42 us (1%)
    all_gather x1, waiting for transfers between devices, shards(): lax.all_gather(jnp.concatenate([keys_local, values_local], axis=0), axis_...  191 us
    unnamed x3, waiting for transfers between devices  36.3 us
    unnamed x26, local copies, waits for them, and re-layouts  26.8 us
    split x1, local copies, waits for them, and re-layouts, shards(): jnp.split(lax.all_gather(jnp.concatenate([keys_local, values_local], axis...  11 us
  transfers between devices with their start and end apart: 3, of which 3 were waited for; matrix products, arithmetic and copies ran while one was open for 1% of the time, Pallas kernels for 0%

profile of v1, /device:TPU:4, one launch (start us, length us, event | category | flops | bytes accessed | tf_op | source)
XLA Modules:
  0.0 324.2 jit_solution(14186076740903343891)
XLA Ops:
  7.2 1.7 convert_multiply_fusion.1
  9.0 1.0 copy.59
  10.0 1.6 convert_multiply_fusion.2
  11.6 1.0 copy.50
  12.6 0.6 fusion.35
  13.2 0.8 slice_bitcast_fusion.2
  14.0 0.8 mul.267
  14.7 1.4 mul.286
  16.2 0.7 convert_multiply_fusion
  16.9 0.1 reduce_sum.36
  17.1 0.1 div.90
  17.2 0.8 fusion.24
  18.0 0.8 copy.53
  18.8 1.7 copy.55
  20.5 1.6 copy.54
  22.0 1.0 mul.285
  23.0 0.2 reduce_sum.38
  23.4 1.0 mul.266
  24.4 0.8 reduce_sum.37
  25.2 1.5 add_sqrt_fusion.1
  26.8 0.9 copy.52
  27.7 0.8 broadcast_multiply_fusion.1
  28.5 0.2 fusion.26
  28.7 1.2 divide_multiply_fusion
  29.9 1.0 subtract_convert_fusion
  30.9 0.5 pad_maximum_fusion
  31.5 0.2 maximum_maximum_fusion
  31.7 0.9 copy.56
  32.7 0.5 pad_maximum_fusion.1
  33.2 0.7 compare_or_fusion
  34.0 190.5 %all-gather.2.cloned.1.call-done = bf16[4,2560,384]{2,0,1:T(4,128)(2,1)} async-done(((bf16[4,80,384]{2,0,1:T(4,128)(2,1)}), bf16[4,2560,384]{2,0,1:T(4,128)(2,1)}) %all-gather.2.cloned.1.call-update) | async-done | bytes 7864336 | tf_op jit(solution)/shard_map/all_gather | solution.py:69
  224.5 11.0 %fusion.38 = (bf16[2,2560,384]{2,0,1:T(2,128)(2,1)}, bf16[2,2560,384]{2,0,1:T(2,128)(2,1)}) fusion(bf16[4,2560,384]{2,0,1:T(4,128)(2,1)} %all-gather.2.cloned.1.call-done), kind=kLoop, calls=%fused_computation.77 | loop fusion | bytes 15728640 | tf_op jit(solution)/shard_map/split | solution.py:68
  235.5 10.5 %copy.73 = bf16[2,2560,384]{1,2,0:T(8,128)(2,1)} copy(bf16[2,2560,384]{2,0,1:T(2,128)(2,1)} %get-tuple-element.2) | data formatting | bytes 7864320
  246.1 5.0 %fusion.39 = (f32[2,64,3]{1,2,0:T(4,128)S(1)}, f32[2,64,3,2560]{3,1,2,0:T(8,128)}) fusion(bf16[2,2560,3,128]{1,3,2,0:T(8,128)(2,1)} %bitcast.68, bf16[2,64,3,128]{1,3,2,0:T(8,128)(2,1)S(1)} %bitcast.77, pred[2,2560]{1,0:T(4,128)(4,1)S(1)} %compare_or_fusion), kind=kOutput, calls=%fused_computation.78 | convolution fusion | flops 254606976 | bytes 7969280 | tf_op jit(solution)/shard_map/pqhd,pkhd->pqhk/dot_general | solution.py:83
  251.1 10.5 %copy.72 = bf16[2,2560,384]{1,2,0:T(8,128)(2,1)} copy(bf16[2,2560,384]{2,0,1:T(2,128)(2,1)} %get-tuple-element.3) | data formatting | bytes 7864320
  261.6 3.1 fusion.2
  264.8 0.2 copy-done.1
  264.9 3.6 %fusion.15 = bf16[2,64,3,128]{3,1,2,0:T(8,128)(2,1)S(1)} fusion(bf16[2,2560,3,128]{1,3,2,0:T(8,128)(2,1)} %bitcast.69, f32[2,64,3,2560]{3,1,2,0:T(8,128)S(1)} %copy-done.1, f32[2,64,3]{1,2,0:T(4,128)S(1)} %broadcast_maximum_fusion, pred[2,2560]{1,0:T(4,128)(4,1)S(1)} %compare_or_fusion, f32[2,64,3]{1,2,0:T(4,128)S(1)} %fusion.2), kind=kOutput, calls=%fused_computation.13 | convolution fusion | flops 254705664 | bytes 7970816 | tf_op jit(solution)/shard_map/pqhk,pkhd->pqhd/dot_general | solution.py:91
  268.6 0.1 copy.65
  268.7 0.6 convolution_convert_fusion
  269.3 1.2 copy.70
  270.5 36.2 %reduce-scatter.4.cloned.1.call-done = bf16[384,128]{1,0:T(8,128)(2,1)} async-done(((bf16[3072,128]{1,0:T(8,128)(2,1)}), bf16[384,128]{1,0:T(8,128)(2,1)}) %reduce-scatter.4.cloned.1.call-update) | async-done | bytes 98320
  306.8 1.0 copy.71
  307.8 0.7 add_convert_fusion
  308.5 3.3 %all-to-all-start = ((bf16[1,2,64,384]{3,2,0,1:T(8,128)(2,1)}), bf16[1,2,64,384]{3,2,0,1:T(8,128)(2,1)S(1)}, u32[]{:S(2)}, u32[]{:S(2)}) async-start(bf16[1,2,64,384]{3,2,0,1:T(8,128)(2,1)} %add_convert_fusion), calls=%async_computation | async-start | bytes 196608 | tf_op jit(solution)/shard_map/all_to_all | solution.py:107
  312.6 0.6 dynamic_slice.3
  313.2 2.9 all-to-all-done
  316.1 1.2 add_convert_fusion.3
  (36 shorter events, 0.4 us)
Async XLA Ops:
  7.2 261.6 %copy-start = (bf16[384,3072]{1,0:T(8,128)(2,1)S(1)}, bf16[384,3072]{1,0:T(8,128)(2,1)}, u32[]{:S(2)}) copy-start(bf16[384,3072]{1,0:T(8,128)(2,1)} %param.24) | copy-start | bytes 7077892
  7.2 217.3 %all-gather.2.cloned.1.call-start = ((), (), s32[]{:S(2)}) async-start(), calls=%async_computation.2 | async-start | bytes 8110080 | tf_op jit(solution)/shard_map/all_gather | solution.py:69
  25.2 6.2 %copy-start.2 = (bf16[2,16,384]{1,2,0:T(8,128)(2,1)S(1)}, bf16[2,16,384]{1,2,0:T(8,128)(2,1)}, u32[]{:S(2)}) copy-start(bf16[2,16,384]{1,2,0:T(8,128)(2,1)} %copy.53) | copy-start | bytes 73732
  25.2 6.2 %copy-start.3 = (bf16[1,2,64,384]{2,3,1,0:T(8,128)(2,1)S(1)}, bf16[1,2,64,384]{2,3,1,0:T(8,128)(2,1)}, u32[]{:S(2)}) copy-start(bf16[1,2,64,384]{2,3,1,0:T(8,128)(2,1)} %copy.55) | copy-start | bytes 294916
  27.7 3.8 %copy-start.4 = (bf16[1,2,16,384]{2,3,1,0:T(8,128)(2,1)S(1)}, bf16[1,2,16,384]{2,3,1,0:T(8,128)(2,1)}, u32[]{:S(2)}) copy-start(bf16[1,2,16,384]{2,3,1,0:T(8,128)(2,1)} %copy.54) | copy-start | bytes 73732
  32.6 274.1 %reduce-scatter.4.cloned.1.call-start = ((), (), s32[]{:S(2)}) async-start(), calls=%async_computation.3 | async-start | bytes 884736
  261.6 3.3 %copy-start.1 = (f32[2,64,3,2560]{3,1,2,0:T(8,128)S(1)}, f32[2,64,3,2560]{3,1,2,0:T(8,128)}, u32[]{:S(2)}) copy-start(f32[2,64,3,2560]{3,1,2,0:T(8,128)} %get-tuple-element.19) | copy-start | bytes 11796484
  268.6 39.2 %copy-start.8 = (f32[384]{0:T(512)S(1)}, f32[384]{0:T(512)}, u32[]{:S(2)}) copy-start(f32[384]{0:T(512)} %param.25) | copy-start | bytes 4612
  268.6 39.2 %copy-start.5 = (bf16[1,2,64,384]{3,2,1,0:T(8,128)(2,1)S(1)}, bf16[1,2,64,384]{3,2,1,0:T(8,128)(2,1)}, u32[]{:S(2)}) copy-start(bf16[1,2,64,384]{3,2,1,0:T(8,128)(2,1)} %param.15) | copy-start | bytes 294916
  268.6 39.2 %copy-start.7 = (f32[1,2,384]{2,1,0:T(2,128)S(1)}, f32[1,2,384]{2,1,0:T(2,128)}, u32[]{:S(2)}) copy-start(f32[1,2,384]{2,1,0:T(2,128)} %param.23) | copy-start | bytes 9220
  268.6 44.0 %copy-start.9 = (f32[2]{0:T(128)S(1)}, f32[2]{0:T(128)}, u32[]{:S(2)}) copy-start(f32[2]{0:T(128)} %param.26) | copy-start | bytes 28
  268.6 47.5 %copy-start.6 = (bf16[1,64,384]{2,1,0:T(8,128)(2,1)S(1)}, bf16[1,64,384]{2,1,0:T(8,128)(2,1)}, u32[]{:S(2)}) copy-start(bf16[1,64,384]{2,1,0:T(8,128)(2,1)} %param.29) | copy-start | bytes 147460
  308.5 7.6 %all-to-all-start = ((bf16[1,2,64,384]{3,2,0,1:T(8,128)(2,1)}), bf16[1,2,64,384]{3,2,0,1:T(8,128)(2,1)S(1)}, u32[]{:S(2)}, u32[]{:S(2)}) async-start(bf16[1,2,64,384]{3,2,0,1:T(8,128)(2,1)} %add_convert_fusion), calls=%async_computation | async-start | bytes 196608 | tf_op jit(solution)/shard_map/all_to_all | solution.py:107
Sparse Core Ops, SparseCore 0:
  32.7 191.6 all-gather.1
  270.6 36.0 reduce-scatter.3
